TPU v7x, 32 devices: a whole 2x2x4 slice. The times are simulated.
32 devices in a mesh: row: 4 (over z), col: 8 (over y, x, core).
Axes of the slice: x: 2, y: 2, z: 4, core: 2. Of those that a mesh axis runs over, the one named last changes fastest.
Arguments:
- amplitudes: bfloat16 [16, 16, 12, 4096], P('row', 'col'), may hold values from -6 to 6
- integrals: bfloat16 [16, 16, 47, 4096], P('row', 'col'), may hold values from -0.1875 to 0.1875
- pair_lists: int32 [4, 12, 2], replicated, may hold values from 0 to 46, as said below
- tile_counts: int32 [4], replicated, may hold values from 1 to 12, as said below
Outputs:
- symmetric: float32 [16, 16, 12, 4096], P('row', 'col')
Inputs may be any that keep to these rules, and one draw needn't show every extreme that they name: `pair_lists`: each grid row lists 12 distinct ordered pairs of different tiles. `tile_counts`: the largest count equals 12.
All inputs are finite; a program needn't handle non-finite values.
Results may differ from a plain program's by a relative error of at most 0.0029.
Values may be sent and summed in bfloat16 or wider, within the bound.
No kernel may reach another device: no remote copies, remote signals or barrier semaphores. Data moves between devices by JAX's collectives and lax.ppermute only.
A program may use at most 128 MiB of HBM per device.

v0:
```python
import jax
import jax.numpy as jnp
from jax import lax
from jax.sharding import PartitionSpec as P

TILE = 64


def mirror_pairs(row_devices, col_devices, step):
    ratio = col_devices // row_devices
    pairs = []
    for row in range(row_devices):
        for col in range(col_devices):
            part = (col % ratio + step) % ratio
            pairs.append((row * col_devices + col, col // ratio * col_devices + row * ratio + part))
    return pairs


def on_device(amplitudes, integrals, pair_lists, tile_counts):
    occ_row, occ_col, slot_count, square = amplitudes.shape
    tile_width = TILE
    row_devices = lax.axis_size("row")
    col_devices = lax.axis_size("col")
    col_ratio = col_devices // row_devices
    my_row = lax.axis_index("row")
    my_col = lax.axis_index("col")
    partner_row = my_col // col_ratio
    tile_first = pair_lists[:, :, 0]
    tile_second = pair_lists[:, :, 1]
    packed = jnp.take(integrals, tile_second.reshape(-1), axis=2)
    packed = packed.reshape(occ_row, occ_col, row_devices, slot_count, square)
    received = lax.all_to_all(packed, "row", split_axis=2, concat_axis=0, tiled=True)
    received = received.reshape(occ_row * row_devices, occ_col, slot_count, square)
    piece = lax.all_gather(amplitudes, "col", axis=1, tiled=True)
    piece_count = piece.shape[1]
    left_tiles = piece.reshape(occ_row, piece_count, slot_count, tile_width, tile_width)
    right_tiles = received.reshape(piece_count, occ_col, slot_count, tile_width, tile_width)
    cycle_sum = jnp.einsum(
        "iksac,kjscb->ijsab", left_tiles, right_tiles, preferred_element_type=jnp.float32
    )
    my_count = lax.dynamic_index_in_dim(tile_counts, my_row, 0, keepdims=False)
    live_slots = (jnp.arange(slot_count, dtype=jnp.int32) < my_count).astype(jnp.float32)
    cycle_value = (cycle_sum * live_slots[None, None, :, None, None]).astype(jnp.bfloat16)
    cycle = cycle_value.reshape(occ_row, occ_col, slot_count, square)
    halves = cycle.reshape(col_ratio, occ_col, occ_col, slot_count, square)
    col_part = lax.rem(my_col, col_ratio)
    arrived = []
    for step in range(col_ratio):
        part = lax.rem(col_part + step, col_ratio)
        block = lax.dynamic_index_in_dim(halves, part, 0, keepdims=False)
        arrived.append(
            lax.ppermute(block, ("row", "col"), mirror_pairs(row_devices, col_devices, step))
        )
    arrived = jnp.stack(arrived)
    order = lax.rem(col_part - jnp.arange(col_ratio) + col_ratio, col_ratio)
    arrived = jnp.take(arrived, order, axis=0)
    mirror_block = jnp.moveaxis(arrived, 0, 1).reshape(occ_col, occ_row, slot_count, square)
    mirror_block = mirror_block.reshape(occ_col, occ_row, slot_count, tile_width, tile_width)
    mine_first = lax.dynamic_index_in_dim(tile_first, my_row, 0, keepdims=False)
    mine_second = lax.dynamic_index_in_dim(tile_second, my_row, 0, keepdims=False)
    their_first = lax.dynamic_index_in_dim(tile_first, partner_row, 0, keepdims=False)
    their_second = lax.dynamic_index_in_dim(tile_second, partner_row, 0, keepdims=False)
    pair_match = (
        (mine_first[:, None] == their_second[None, :])
        & (mine_second[:, None] == their_first[None, :])
    ).astype(jnp.bfloat16)
    crossed = jnp.einsum(
        "st,jitba->ijsab", pair_match, mirror_block, preferred_element_type=jnp.float32
    )
    own_part = cycle_value.astype(jnp.float32)
    symmetric = (own_part + crossed) * live_slots[None, None, :, None, None]
    return symmetric.reshape(occ_row, occ_col, slot_count, square)


def solution(mesh):
    return jax.shard_map(
        on_device,
        mesh=mesh,
        in_specs=(P("row", "col", None, None), P("row", "col", None, None), P(), P()),
        out_specs=P("row", "col", None, None),
        check_vma=False,
    )
```

profile of v0, /device:TPU:3, one launch (start us, length us, event | category | flops | bytes accessed | tf_op | source)
XLA Modules:
  0.0 234.9 jit_solution(8737630853103244513)
XLA Ops:
  6.5 0.0 copy-start
  6.5 0.0 all-gather.2.cloned.1.call-start
  6.5 2.8 %copy.23 = bf16[4,2,12,4096]{3,0,2,1:T(4,128)(2,1)} copy(bf16[4,2,12,4096]{3,1,2,0:T(2,128)(2,1)} %param.4) | data formatting | bytes 1572864 | tf_op args[0]
  9.3 0.0 all-gather.2.cloned.1.call-update
  9.3 0.8 fusion.33
  10.1 0.1 reshape_squeeze.6
  10.2 0.0 copy-done
  10.2 8.5 %gather_fusion = bf16[48,4,2,4096]{3,2,1,0:T(2,128)(2,1)} fusion(bf16[4,2,47,4096]{3,1,2,0:T(2,128)(2,1)S(1)} %copy-done, s32[1024]{0:T(1024)S(1)} %pad_clamp_fusion.1), kind=kCustom, calls=%fused_computation | custom fusion | bytes 6291648 | tf_op jit(solution)/shard_map/jit(_take)/gather | solution.py:30
  18.7 6.6 %broadcast_select_fusion = bf16[4,2,4,12,4096]{4,1,3,0,2:T(2,128)(2,1)} fusion(pred[4,12]{1,0:T(4,128)(4,1)S(1)} %compare_and_fusion.1, bf16[4,2,4,12,4096]{4,1,0,3,2:T(2,128)(2,1)} %bitcast.73), kind=kLoop, calls=%fused_computation.5 | loop fusion | flops 1572864 | bytes 6291504 | tf_op jit(solution)/shard_map/jit(_take)/select_n | solution.py:30
  25.4 0.0 copy-start.4
  25.4 5.0 %all-to-all-start = ((bf16[4,2,4,12,4096]{4,1,3,0,2:T(2,128)(2,1)}), bf16[4,2,4,12,4096]{4,1,3,0,2:T(2,128)(2,1)}, u32[]{:S(2)}, u32[]{:S(2)}) async-start(bf16[4,2,4,12,4096]{4,1,3,0,2:T(2,128)(2,1)} %broadcast_select_fusion), calls=%async_computation | async-start | bytes 6291456 | tf_op jit(solution)/shard_map/all_to_all | solution.py:32
  30.4 0.0 copy-done.4
  30.4 0.6 dynamic_slice.24
  31.0 0.6 compare_convert_fusion
  31.7 69.0 %all-to-all-done = bf16[4,2,4,12,4096]{4,1,3,0,2:T(2,128)(2,1)} async-done(((bf16[4,2,4,12,4096]{4,1,3,0,2:T(2,128)(2,1)}), bf16[4,2,4,12,4096]{4,1,3,0,2:T(2,128)(2,1)}, u32[]{:S(2)}, u32[]{:S(2)}) %all-to-all-start) | async-done | bytes 3145760 | tf_op jit(solution)/shard_map/all_to_all | solution.py:32
  100.6 11.1 %reshape_reshape.9 = bf16[16,2,12,64,64]{4,3,1,2,0:T(8,128)(2,1)} reshape(bf16[4,4,2,1,12,4096]{5,2,4,1,0,3:T(2,128)(2,1)} %bitcast.5) | data formatting | bytes 6291456 | tf_op jit(solution)/shard_map/reshape;reshape | solution.py:37
  111.7 0.0 all-gather.2.cloned.1.call-done
  111.7 9.3 %copy.24 = bf16[4,16,12,4096]{3,1,0,2:T(8,128)(2,1)} copy(bf16[4,16,12,4096]{3,0,2,1:T(4,128)(2,1)} %all-gather.2.cloned.1.call-done) | data formatting | bytes 12582912 | tf_op jit(solution)/shard_map/all_gather | solution.py:34
  121.1 17.9 %reshape.123 = bf16[4,16,12,64,64,1]{4,3,1,0,2,5:T(8,128)(2,1)} reshape(bf16[4,16,12,4096]{3,1,0,2:T(8,128)(2,1)} %copy.24) | data formatting | bytes 12582912 | tf_op jit(solution)/shard_map/reshape | solution.py:36
  139.0 11.1 %fusion.11 = bf16[4,2,12,64,64]{3,4,0,1,2:T(8,128)(2,1)S(1)} fusion(f32[12]{0:T(128)S(1)} %compare_convert_fusion, bf16[4,16,12,64,64,1]{4,3,1,0,2,5:T(8,128)(2,1)} %reshape.123, bf16[16,2,12,64,64]{4,3,1,2,0:T(8,128)(2,1)} %reshape_reshape.9), kind=kOutput, calls=%fused_computation.13 | convolution fusion | flops 806092800 | bytes 10223664 | tf_op jit(solution)/shard_map/iksac,kjscb->ijsab/dot_general | solution.py:38
  150.1 0.0 copy-start.2
  150.1 1.7 copy.26
  151.8 3.1 %reshape_reshape.10 = bf16[2,2,2,12,4096]{4,2,3,1,0:T(2,128)(2,1)S(1)} reshape(bf16[4,2,12,64,64]{4,3,1,2,0:T(8,128)(2,1)} %copy.26) | data formatting | bytes 1572864 | tf_op jit(solution)/shard_map/reshape;reshape | solution.py:45
  154.9 0.8 dynamic-slice_bitcast_fusion.1
  155.7 0.0 copy-done.2
  155.7 0.1 collective-permute-start.1
  155.8 5.8 %collective-permute-start = (bf16[2,2,12,4096]{3,1,2,0:T(2,128)(2,1)S(1)}, bf16[2,2,12,4096]{3,1,2,0:T(2,128)(2,1)S(1)}, u32[]{:S(2)}, u32[]{:S(2)}) collective-permute-start(bf16[2,2,12,4096]{3,1,2,0:T(2,128)(2,1)S(1)} %get-tuple-element.5), channel_id=1, source_target_pairs={{0,0},{1,1},{2,8},{3,9},{4,16},{5,17},{6,24},{7,25},{8,2},{9,3},{1... | collective-permute-start | bytes 1179656 | tf_op jit(solution)/shard_map/ppermute | solution.py:52
  161.7 39.6 %collective-permute-done.1 = bf16[2,2,12,4096]{3,1,2,0:T(2,128)(2,1)S(1)} collective-permute-done((bf16[2,2,12,4096]{3,1,2,0:T(2,128)(2,1)S(1)}, bf16[2,2,12,4096]{3,1,2,0:T(2,128)(2,1)S(1)}, u32[]{:S(2)}, u32[]{:S(2)}) %collective-permute-start.1) | collective-permute-done | bytes 393248 | tf_op jit(solution)/shard_map/ppermute | solution.py:52
  201.3 8.9 %collective-permute-done = bf16[2,2,12,4096]{3,1,2,0:T(2,128)(2,1)S(1)} collective-permute-done((bf16[2,2,12,4096]{3,1,2,0:T(2,128)(2,1)S(1)}, bf16[2,2,12,4096]{3,1,2,0:T(2,128)(2,1)S(1)}, u32[]{:S(2)}, u32[]{:S(2)}) %collective-permute-start) | collective-permute-done | bytes 393248 | tf_op jit(solution)/shard_map/ppermute | solution.py:52
  210.2 1.1 pad_maximum_fusion
  211.4 2.1 gather_fusion.1
  213.5 0.7 fusion.16
  214.2 0.8 copy.27
  215.0 1.0 reshape_reshape.11
  216.1 0.0 copy-start.3
  216.1 1.1 fusion.5
  217.2 0.3 copy-done.3
  217.5 2.7 %fusion.3 = f32[4,2,12,64,64]{3,4,0,1,2:T(8,128)} fusion(f32[2,4,64,64,12]{3,4,2,1,0:T(8,128)S(1)} %fusion.5, bf16[4,2,12,64,64]{3,4,0,1,2:T(8,128)(2,1)S(1)} %copy-done.3, f32[12]{0:T(128)S(1)} %compare_convert_fusion), kind=kLoop, calls=%fused_computation.7 | loop fusion | flops 1179648 | bytes 3932208 | tf_op jit(solution)/shard_map/mul | solution.py:71
  220.2 0.0 copy-start.1
  220.2 3.7 %copy.30 = f32[4,2,12,64,64]{4,3,1,2,0:T(8,128)} copy(f32[4,2,12,64,64]{3,4,0,1,2:T(8,128)} %fusion.3) | data formatting | bytes 3145728 | tf_op jit(solution)/shard_map/mul | solution.py:71
  223.9 4.2 %reshape.105 = f32[4,2,12,4096]{3,1,2,0:T(2,128)} reshape(f32[4,2,12,64,64]{4,3,1,2,0:T(8,128)} %copy.30) | data formatting | bytes 3145728 | tf_op jit(solution)/shard_map/reshape | solution.py:72
  228.1 0.0 copy-done.1
  (7 shorter events, 0.1 us)
Async XLA Ops:
  6.5 3.7 %copy-start = (bf16[4,2,47,4096]{3,1,2,0:T(2,128)(2,1)S(1)}, bf16[4,2,47,4096]{3,1,2,0:T(2,128)(2,1)}, u32[]{:S(2)}) copy-start(bf16[4,2,47,4096]{3,1,2,0:T(2,128)(2,1)} %param.5) | copy-start | bytes 9240580
  6.5 105.2 %all-gather.2.cloned.1.call-start = ((), (), s32[]{:S(2)}) async-start(), calls=%async_computation.1 | async-start | bytes 7077888 | tf_op jit(solution)/shard_map/all_gather | solution.py:34
  25.4 5.0 %copy-start.4 = (s32[4]{0:T(128)S(1)}, s32[4]{0:T(128)}, u32[]{:S(2)}) copy-start(s32[4]{0:T(128)} %param.7) | copy-start | bytes 52
  25.4 75.3 %all-to-all-start = ((bf16[4,2,4,12,4096]{4,1,3,0,2:T(2,128)(2,1)}), bf16[4,2,4,12,4096]{4,1,3,0,2:T(2,128)(2,1)}, u32[]{:S(2)}, u32[]{:S(2)}) async-start(bf16[4,2,4,12,4096]{4,1,3,0,2:T(2,128)(2,1)} %broadcast_select_fusion), calls=%async_computation | async-start | bytes 6291456 | tf_op jit(solution)/shard_map/all_to_all | solution.py:32
  150.1 5.6 %copy-start.2 = (bf16[4,2,12,64,64]{3,4,0,1,2:T(8,128)(2,1)}, bf16[4,2,12,64,64]{3,4,0,1,2:T(8,128)(2,1)S(1)}, u32[]{:S(2)}) copy-start(bf16[4,2,12,64,64]{3,4,0,1,2:T(8,128)(2,1)S(1)} %fusion.11) | copy-start | bytes 2359300
  155.7 45.6 %collective-permute-start.1 = (bf16[2,2,12,4096]{3,1,2,0:T(2,128)(2,1)S(1)}, bf16[2,2,12,4096]{3,1,2,0:T(2,128)(2,1)S(1)}, u32[]{:S(2)}, u32[]{:S(2)}) collective-permute-start(bf16[2,2,12,4096]{3,1,2,0:T(2,128)(2,1)S(1)} %get-tuple-element.6), channel_id=1, source_target_pairs={{0,1},{1,0},{2,9},{3,8},{4,17},{5,16},{6,25},{7,24},{8,3},{9,2},{1... | collective-permute-start | bytes 1179656 | tf_op jit(solution)/shard_map/ppermute | solution.py:52
  155.8 54.4 %collective-permute-start = (bf16[2,2,12,4096]{3,1,2,0:T(2,128)(2,1)S(1)}, bf16[2,2,12,4096]{3,1,2,0:T(2,128)(2,1)S(1)}, u32[]{:S(2)}, u32[]{:S(2)}) collective-permute-start(bf16[2,2,12,4096]{3,1,2,0:T(2,128)(2,1)S(1)} %get-tuple-element.5), channel_id=1, source_target_pairs={{0,0},{1,1},{2,8},{3,9},{4,16},{5,17},{6,24},{7,25},{8,2},{9,3},{1... | collective-permute-start | bytes 1179656 | tf_op jit(solution)/shard_map/ppermute | solution.py:52
  216.1 1.4 copy-start.3
  220.2 7.9 %copy-start.1 = (bf16[4,2,47,4096]{3,1,2,0:T(2,128)(2,1)S(1)}, bf16[4,2,47,4096]{3,1,2,0:T(2,128)(2,1)}, u32[]{:S(2)}) copy-start(bf16[4,2,47,4096]{3,1,2,0:T(2,128)(2,1)} %param.5) | copy-start | bytes 9240580
Sparse Core Ops, SparseCore 0:
  9.5 47.0 all-gather.1
where the time goes:
time: 236 us; the launch traced here: 235 us
  waiting for transfers between devices  118 us (50%)
  local copies, waits for them, and re-layouts  68.9 us (29%)
  between operations  13.6 us (6%)
  matrix products  12.2 us (5%)
  other arithmetic  11.9 us (5%)
  starting transfers between devices  10.9 us (5%)
    all_to_all x1, waiting for transfers between devices, on_device(): lax.all_to_all(packed, 'row', split_axis=2, concat_axis=0, tiled=True)  69 us
    ppermute x2, waiting for transfers between devices, on_device(): lax.ppermute(block, ('row', 'col'), mirror_pairs(row_devices, col_devices...  48.5 us
    reshape x1, local copies, waits for them, and re-layouts, on_device(): piece.reshape(occ_row, piece_count, slot_count, tile_width, tile_width)  17.9 us
    another operation x1, local copies, waits for them, and re-layouts, on_device(): received.reshape(piece_count, occ_col, slot_count, tile_width, tile_width)  11.1 us
    dot_general x1, matrix products, on_device(): jnp.einsum('iksac,kjscb->ijsab', left_tiles, right_tiles, preferred_eleme...  11.1 us
    all_gather x1, local copies, waits for them, and re-layouts, on_device(): piece = lax.all_gather(amplitudes, 'col', axis=1, tiled=True)  9.34 us
    gather x1, local copies, waits for them, and re-layouts, on_device(): packed = jnp.take(integrals, tile_second.reshape(-1), axis=2)  8.51 us
    select_n x2, other arithmetic, on_device(): packed = jnp.take(integrals, tile_second.reshape(-1), axis=2)  6.63 us
  transfers between devices with their start and end apart: 4, of which 3 were waited for; matrix products, arithmetic and copies ran while one was open for 12% of the time, Pallas kernels for 0%

commit v1 on v0

--- a/solution.py
+++ b/solution.py
@@ -4,6 +4,17 @@
 from jax.sharding import PartitionSpec as P
 
 TILE = 64
+
+
+def in_blocks(x, dim, count):
+    before, after = (x.shape[:dim], x.shape[dim + 1 :])
+    return jnp.moveaxis(x.reshape(*before, count, -1, *after), dim, 0)
+
+
+def joined_along(blocks, dim):
+    blocks = jnp.moveaxis(blocks, 0, dim)
+    shape = blocks.shape
+    return blocks.reshape(*shape[:dim], shape[dim] * shape[dim + 1], *shape[dim + 2 :])
 
 
 def mirror_pairs(row_devices, col_devices, step):
@@ -29,7 +40,14 @@
     tile_second = pair_lists[:, :, 1]
     packed = jnp.take(integrals, tile_second.reshape(-1), axis=2)
     packed = packed.reshape(occ_row, occ_col, row_devices, slot_count, square)
-    received = lax.all_to_all(packed, "row", split_axis=2, concat_axis=0, tiled=True)
+    peers, mine = (lax.axis_size("row"), lax.axis_index("row"))
+    parts = in_blocks(packed, 2, peers)
+    finished = [parts[mine]]
+    for turn in range(1, peers):
+        sent = parts[mine ^ turn]
+        finished.append(lax.ppermute(sent, "row", [(i, i ^ turn) for i in range(peers)]))
+    parts = jnp.stack(finished)[mine ^ jnp.arange(peers)]
+    received = joined_along(parts, 0)
     received = received.reshape(occ_row * row_devices, occ_col, slot_count, square)
     piece = lax.all_gather(amplitudes, "col", axis=1, tiled=True)
     piece_count = piece.shape[1]

time: 236 us -> 252 us (1.068)
  local copies, waits for them, and re-layouts: 68.9 us -> 85.2 us
  other arithmetic: 11.9 us -> 16.7 us
  waiting for transfers between devices: 118 us -> 115 us
    all_to_all x1 -> x0, waiting for transfers between devices: 69 us -> none  [on_device(): lax.all_to_all(packed, 'row', split_axis=2, concat_axis=0, tiled=True)]
    ppermute x0 -> x3, waiting for transfers between devices: none -> 65.7 us  [on_device(): lax.ppermute(sent, 'row', [(i, i ^ turn) for i in range(peers)])]
    gather x0 -> x2, local copies, waits for them, and re-layouts: none -> 13.5 us  [on_device(): parts = jnp.stack(finished)[mine ^ jnp.arange(peers)]]
    another operation x0 -> x1, other arithmetic: none -> 5.08 us  [on_device(): parts = jnp.stack(finished)[mine ^ jnp.arange(peers)]]
    all_to_all x1 -> x0, starting transfers between devices: 4.97 us -> none  [on_device(): lax.all_to_all(packed, 'row', split_axis=2, concat_axis=0, tiled=True)]
    ppermute x0 -> x3, starting transfers between devices: none -> 3.63 us  [on_device(): lax.ppermute(sent, 'row', [(i, i ^ turn) for i in range(peers)])]
    dynamic_slice x0 -> x1, local copies, waits for them, and re-layouts: none -> 2.58 us  [on_device(): finished = [parts[mine]]]
  transfers between devices with their start and end apart: 4 -> 6, of which waited for: 3 -> 4; matrix products, arithmetic and copies ran while one was open for 12% -> 20% of each run, Pallas kernels for 0% -> 0%
where the time goes in v1:
time: 252 us; the launch traced here: 251 us
  waiting for transfers between devices  115 us (46%)
  local copies, waits for them, and re-layouts  85.2 us (34%)
  other arithmetic  16.7 us (7%)
  between operations  13.6 us (5%)
  matrix products  12.2 us (5%)
  starting transfers between devices  9.18 us (4%)
    ppermute x3, waiting for transfers between devices, on_device(): lax.ppermute(sent, 'row', [(i, i ^ turn) for i in range(peers)])  65.7 us
    ppermute x2, waiting for transfers between devices, on_device(): lax.ppermute(block, ('row', 'col'), mirror_pairs(row_devices, col_devices...  48.9 us
    reshape x1, local copies, waits for them, and re-layouts, on_device(): piece.reshape(occ_row, piece_count, slot_count, tile_width, tile_width)  17.9 us
    gather x2, local copies, waits for them, and re-layouts, on_device(): parts = jnp.stack(finished)[mine ^ jnp.arange(peers)]  13.5 us
    another operation x1, local copies, waits for them, and re-layouts, on_device(): received.reshape(piece_count, occ_col, slot_count, tile_width, tile_width)  11.1 us
    dot_general x1, matrix products, on_device(): jnp.einsum('iksac,kjscb->ijsab', left_tiles, right_tiles, preferred_eleme...  11.1 us
    all_gather x1, local copies, waits for them, and re-layouts, on_device(): piece = lax.all_gather(amplitudes, 'col', axis=1, tiled=True)  9.35 us
    gather x1, local copies, waits for them, and re-layouts, on_device(): packed = jnp.take(integrals, tile_second.reshape(-1), axis=2)  8.51 us
  transfers between devices with their start and end apart: 6, of which 4 were waited for; matrix products, arithmetic and copies ran while one was open for 20% of the time, Pallas kernels for 0%

profile of v1, /device:TPU:3, one launch (start us, length us, event | category | flops | bytes accessed | tf_op | source)
XLA Modules:
  0.0 251.4 jit_solution(1225807522598140988)
XLA Ops:
  6.5 0.0 copy-start
  6.5 0.0 all-gather.2.cloned.1.call-start
  6.5 2.8 %copy.24 = bf16[4,2,12,4096]{3,0,2,1:T(4,128)(2,1)} copy(bf16[4,2,12,4096]{3,1,2,0:T(2,128)(2,1)} %param.4) | data formatting | bytes 1572864 | tf_op args[0]
  9.3 0.0 all-gather.2.cloned.1.call-update
  9.4 0.8 fusion.34
  10.1 0.1 reshape_squeeze.6
  10.2 0.0 copy-done
  10.3 8.5 %gather_fusion = bf16[48,4,2,4096]{3,2,1,0:T(2,128)(2,1)} fusion(bf16[4,2,47,4096]{3,1,2,0:T(2,128)(2,1)S(1)} %copy-done, s32[1024]{0:T(1024)S(1)} %pad_clamp_fusion.2), kind=kCustom, calls=%fused_computation | custom fusion | bytes 6291648 | tf_op jit(solution)/shard_map/jit(_take)/gather | solution.py:41
  18.8 6.4 %copy_select_fusion = bf16[4,2,4,1,12,4096]{5,0,4,1,3,2:T(4,128)(2,1)S(1)} fusion(bf16[4,2,4,1,12,4096]{5,1,0,4,2,3:T(2,128)(2,1)} %bitcast.85, pred[4,12]{1,0:T(4,128)(4,1)S(1)} %compare_and_fusion.1), kind=kLoop, calls=%fused_computation.11 | loop fusion | flops 1572864 | bytes 6291504 | tf_op jit(solution)/shard_map/jit(_take)/select_n | solution.py:41
  25.2 0.0 copy-start.4
  25.2 2.6 %dynamic-slice_bitcast_fusion.3 = (bf16[1,4,2,1,12,4096]{5,1,4,2,0,3:T(4,128)(2,1)S(1)}, bf16[4,2,1,12,4096]{4,0,3,1,2:T(4,128)(2,1)}, bf16[4,2,1,12,4096]{4,0,3,1,2:T(4,128)(2,1)}, bf16[4,2,1,12,4096]{4,0,3,1,2:T(4,128)(2,1)}) fusion(bf16[4,2,4,1,12,4096]{5,0,4,1,3,2:T(4,128)(2,1)S(1)} %copy_select_fusion, s32[]{:T(128)S(6)} %select_n.98, ...), kind=kLoop, calls=%fused_computation.20 | loop fusion | bytes 6291472 | tf_op jit(solution)/shard_map/dynamic_slice | solution.py:45
  27.8 3.3 %collective-permute-start.2 = (bf16[4,2,1,12,4096]{4,0,3,1,2:T(4,128)(2,1)}, bf16[4,2,1,12,4096]{4,0,3,1,2:T(4,128)(2,1)S(1)}, u32[]{:S(2)}, u32[]{:S(2)}) collective-permute-start(bf16[4,2,1,12,4096]{4,0,3,1,2:T(4,128)(2,1)} %get-tuple-element.6), channel_id=1, source_target_pairs={{0,24},{8,16},{16,8},{24,0},{1,25},{9,17},{17,9},{25,1},{2,26},{10... | collective-permute-start | bytes 2359304 | tf_op jit(solution)/shard_map/ppermute | solution.py:48
  31.1 0.0 collective-permute-start.1
  31.1 0.3 collective-permute-start
  31.4 0.0 copy-done.4
  31.4 0.6 dynamic_slice.31
  32.0 0.5 compare_convert_fusion
  32.5 16.0 %collective-permute-done.2 = bf16[4,2,1,12,4096]{4,0,3,1,2:T(4,128)(2,1)S(1)} collective-permute-done((bf16[4,2,1,12,4096]{4,0,3,1,2:T(4,128)(2,1)}, bf16[4,2,1,12,4096]{4,0,3,1,2:T(4,128)(2,1)S(1)}, u32[]{:S(2)}, u32[]{:S(2)}) %collective-permute-start.2) | collective-permute-done | bytes 786464 | tf_op jit(solution)/shard_map/ppermute | solution.py:48
  48.5 49.7 %collective-permute-done.1 = bf16[4,2,1,12,4096]{4,0,3,1,2:T(4,128)(2,1)S(1)} collective-permute-done((bf16[4,2,1,12,4096]{4,0,3,1,2:T(4,128)(2,1)}, bf16[4,2,1,12,4096]{4,0,3,1,2:T(4,128)(2,1)S(1)}, u32[]{:S(2)}, u32[]{:S(2)}) %collective-permute-start.1) | collective-permute-done | bytes 786464 | tf_op jit(solution)/shard_map/ppermute | solution.py:48
  98.2 0.0 collective-permute-done
  98.2 5.1 %maximum_bitcast_fusion = bf16[4,4,2,12,4096]{4,1,3,2,0:T(4,128)(2,1)} fusion(bf16[1,4,2,1,12,4096]{5,1,4,2,0,3:T(4,128)(2,1)S(1)} %bitcast.86, bf16[1,4,2,1,12,4096]{5,1,4,2,0,3:T(4,128)(2,1)S(1)} %bitcast.87, bf16[1,4,2,1,12,4096]{5,1,4,2,0,3:T(4,128)(2,1)} %bitcast.6, bf16[1,4,2,1,12,4096]{5,1,4,2,0,3:T(4,128)(2,1)S(1)} %get-tuple-element.5), kind=kLoop, calls=%fused_computation.6 | loop fusion | flops 4718592 | bytes 6291456 | tf_op jit(solution)/shard_map/stack | solution.py:49
  103.3 6.6 %gather_fusion.1 = bf16[4,4,2,12,4096]{4,1,3,2,0:T(4,128)(2,1)} fusion(bf16[4,4,2,12,4096]{4,1,3,2,0:T(4,128)(2,1)} %maximum_bitcast_fusion, s32[1024]{0:T(1024)S(1)} %pad_clamp_fusion.1), kind=kCustom, calls=%fused_computation.1 | custom fusion | bytes 6291472 | tf_op jit(solution)/shard_map/gather | solution.py:49
  109.9 6.9 %copy.23 = bf16[4,4,2,12,4096]{4,2,3,1,0:T(2,128)(2,1)} copy(bf16[4,4,2,12,4096]{4,1,3,2,0:T(4,128)(2,1)} %gather_fusion.1) | data formatting | bytes 6291456 | tf_op jit(solution)/shard_map/gather | solution.py:49
  116.8 11.1 %reshape_reshape_reshape.3 = bf16[16,2,12,64,64]{4,3,1,2,0:T(8,128)(2,1)} reshape(bf16[4,4,2,12,4096]{4,2,3,1,0:T(2,128)(2,1)} %copy.23) | data formatting | bytes 6291456 | tf_op jit(solution)/shard_map/reshape;reshape;reshape | solution.py:55
  127.9 9.4 %copy.25 = bf16[4,16,12,4096]{3,1,0,2:T(8,128)(2,1)} copy(bf16[4,16,12,4096]{3,0,2,1:T(4,128)(2,1)} %all-gather.2.cloned.1.call-done) | data formatting | bytes 12582912 | tf_op jit(solution)/shard_map/all_gather | solution.py:52
  137.2 17.9 %reshape.166 = bf16[4,16,12,64,64,1]{4,3,1,0,2,5:T(8,128)(2,1)} reshape(bf16[4,16,12,4096]{3,1,0,2:T(8,128)(2,1)} %copy.25) | data formatting | bytes 12582912 | tf_op jit(solution)/shard_map/reshape | solution.py:54
  155.2 11.1 %fusion.11 = bf16[4,2,12,64,64]{3,4,0,1,2:T(8,128)(2,1)S(1)} fusion(f32[12]{0:T(128)S(1)} %compare_convert_fusion, bf16[4,16,12,64,64,1]{4,3,1,0,2,5:T(8,128)(2,1)} %reshape.166, bf16[16,2,12,64,64]{4,3,1,2,0:T(8,128)(2,1)} %reshape_reshape_reshape.3), kind=kOutput, calls=%fused_computation.15 | convolution fusion | flops 806092800 | bytes 10223664 | tf_op jit(solution)/shard_map/iksac,kjscb->ijsab/dot_general | solution.py:56
  166.3 0.0 copy-start.2
  166.3 1.7 copy.27
  168.0 3.1 %reshape_reshape.7 = bf16[2,2,2,12,4096]{4,2,3,1,0:T(2,128)(2,1)S(1)} reshape(bf16[4,2,12,64,64]{4,3,1,2,0:T(8,128)(2,1)} %copy.27) | data formatting | bytes 1572864 | tf_op jit(solution)/shard_map/reshape;reshape | solution.py:63
  171.1 0.8 dynamic-slice_bitcast_fusion.5
  171.9 0.0 copy-done.2
  171.9 0.8 collective-permute-start.4
  172.7 4.8 %collective-permute-start.3 = (bf16[2,2,12,4096]{3,1,2,0:T(2,128)(2,1)S(1)}, bf16[2,2,12,4096]{3,1,2,0:T(2,128)(2,1)S(1)}, u32[]{:S(2)}, u32[]{:S(2)}) collective-permute-start(bf16[2,2,12,4096]{3,1,2,0:T(2,128)(2,1)S(1)} %get-tuple-element.9), channel_id=1, source_target_pairs={{0,0},{1,1},{2,8},{3,9},{4,16},{5,17},{6,24},{7,25},{8,2},{9,3},{1... | collective-permute-start | bytes 1179656 | tf_op jit(solution)/shard_map/ppermute | solution.py:70
  177.6 40.1 %collective-permute-done.4 = bf16[2,2,12,4096]{3,1,2,0:T(2,128)(2,1)S(1)} collective-permute-done((bf16[2,2,12,4096]{3,1,2,0:T(2,128)(2,1)S(1)}, bf16[2,2,12,4096]{3,1,2,0:T(2,128)(2,1)S(1)}, u32[]{:S(2)}, u32[]{:S(2)}) %collective-permute-start.4) | collective-permute-done | bytes 393248 | tf_op jit(solution)/shard_map/ppermute | solution.py:70
  217.7 8.8 %collective-permute-done.3 = bf16[2,2,12,4096]{3,1,2,0:T(2,128)(2,1)S(1)} collective-permute-done((bf16[2,2,12,4096]{3,1,2,0:T(2,128)(2,1)S(1)}, bf16[2,2,12,4096]{3,1,2,0:T(2,128)(2,1)S(1)}, u32[]{:S(2)}, u32[]{:S(2)}) %collective-permute-start.3) | collective-permute-done | bytes 393248 | tf_op jit(solution)/shard_map/ppermute | solution.py:70
  226.4 1.1 pad_maximum_fusion
  227.6 2.1 gather_fusion.2
  229.7 0.7 fusion.16
  230.4 0.8 copy.28
  231.2 1.3 reshape_reshape.8
  232.5 0.0 copy-start.3
  232.5 1.1 fusion.5
  233.6 0.3 copy-done.3
  233.9 2.7 %fusion.3 = f32[4,2,12,64,64]{3,4,0,1,2:T(8,128)} fusion(f32[2,4,64,64,12]{3,4,2,1,0:T(8,128)S(1)} %fusion.5, bf16[4,2,12,64,64]{3,4,0,1,2:T(8,128)(2,1)S(1)} %copy-done.3, f32[12]{0:T(128)S(1)} %compare_convert_fusion), kind=kLoop, calls=%fused_computation.8 | loop fusion | flops 1179648 | bytes 3932208 | tf_op jit(solution)/shard_map/mul | solution.py:89
  236.6 3.7 %copy.31 = f32[4,2,12,64,64]{4,3,1,2,0:T(8,128)} copy(f32[4,2,12,64,64]{3,4,0,1,2:T(8,128)} %fusion.3) | data formatting | bytes 3145728 | tf_op jit(solution)/shard_map/mul | solution.py:89
  240.4 4.2 %reshape.137 = f32[4,2,12,4096]{3,1,2,0:T(2,128)} reshape(f32[4,2,12,64,64]{4,3,1,2,0:T(8,128)} %copy.31) | data formatting | bytes 3145728 | tf_op jit(solution)/shard_map/reshape | solution.py:90
  244.5 0.0 copy-done.1
  (11 shorter events, 0.1 us)
Async XLA Ops:
  6.5 3.7 %copy-start = (bf16[4,2,47,4096]{3,1,2,0:T(2,128)(2,1)S(1)}, bf16[4,2,47,4096]{3,1,2,0:T(2,128)(2,1)}, u32[]{:S(2)}) copy-start(bf16[4,2,47,4096]{3,1,2,0:T(2,128)(2,1)} %param.5) | copy-start | bytes 9240580
  6.5 121.4 %all-gather.2.cloned.1.call-start = ((), (), s32[]{:S(2)}) async-start(), calls=%async_computation | async-start | bytes 7077888 | tf_op jit(solution)/shard_map/all_gather | solution.py:52
  25.2 6.2 %copy-start.4 = (s32[4]{0:T(128)S(1)}, s32[4]{0:T(128)}, u32[]{:S(2)}) copy-start(s32[4]{0:T(128)} %param.7) | copy-start | bytes 52
  27.8 20.7 %collective-permute-start.2 = (bf16[4,2,1,12,4096]{4,0,3,1,2:T(4,128)(2,1)}, bf16[4,2,1,12,4096]{4,0,3,1,2:T(4,128)(2,1)S(1)}, u32[]{:S(2)}, u32[]{:S(2)}) collective-permute-start(bf16[4,2,1,12,4096]{4,0,3,1,2:T(4,128)(2,1)} %get-tuple-element.6), channel_id=1, source_target_pairs={{0,24},{8,16},{16,8},{24,0},{1,25},{9,17},{17,9},{25,1},{2,26},{10... | collective-permute-start | bytes 2359304 | tf_op jit(solution)/shard_map/ppermute | solution.py:48
  31.1 67.1 %collective-permute-start.1 = (bf16[4,2,1,12,4096]{4,0,3,1,2:T(4,128)(2,1)}, bf16[4,2,1,12,4096]{4,0,3,1,2:T(4,128)(2,1)S(1)}, u32[]{:S(2)}, u32[]{:S(2)}) collective-permute-start(bf16[4,2,1,12,4096]{4,0,3,1,2:T(4,128)(2,1)} %get-tuple-element.7), channel_id=1, source_target_pairs={{0,16},{8,24},{16,0},{24,8},{1,17},{9,25},{17,1},{25,9},{2,18},{10... | collective-permute-start | bytes 2359304 | tf_op jit(solution)/shard_map/ppermute | solution.py:48
  31.1 67.1 %collective-permute-start = (bf16[4,2,1,12,4096]{4,0,3,1,2:T(4,128)(2,1)}, bf16[4,2,1,12,4096]{4,0,3,1,2:T(4,128)(2,1)}, u32[]{:S(2)}, u32[]{:S(2)}) collective-permute-start(bf16[4,2,1,12,4096]{4,0,3,1,2:T(4,128)(2,1)} %get-tuple-element.8), channel_id=1, source_target_pairs={{0,8},{8,0},{16,24},{24,16},{1,9},{9,1},{17,25},{25,17},{2,10},{10... | collective-permute-start | bytes 2359304 | tf_op jit(solution)/shard_map/ppermute | solution.py:48
  166.3 5.6 %copy-start.2 = (bf16[4,2,12,64,64]{3,4,0,1,2:T(8,128)(2,1)}, bf16[4,2,12,64,64]{3,4,0,1,2:T(8,128)(2,1)S(1)}, u32[]{:S(2)}) copy-start(bf16[4,2,12,64,64]{3,4,0,1,2:T(8,128)(2,1)S(1)} %fusion.11) | copy-start | bytes 2359300
  171.9 45.7 %collective-permute-start.4 = (bf16[2,2,12,4096]{3,1,2,0:T(2,128)(2,1)S(1)}, bf16[2,2,12,4096]{3,1,2,0:T(2,128)(2,1)S(1)}, u32[]{:S(2)}, u32[]{:S(2)}) collective-permute-start(bf16[2,2,12,4096]{3,1,2,0:T(2,128)(2,1)S(1)} %get-tuple-element.10), channel_id=1, source_target_pairs={{0,1},{1,0},{2,9},{3,8},{4,17},{5,16},{6,25},{7,24},{8,3},{9,2},{1... | collective-permute-start | bytes 1179656 | tf_op jit(solution)/shard_map/ppermute | solution.py:70
  172.7 53.8 %collective-permute-start.3 = (bf16[2,2,12,4096]{3,1,2,0:T(2,128)(2,1)S(1)}, bf16[2,2,12,4096]{3,1,2,0:T(2,128)(2,1)S(1)}, u32[]{:S(2)}, u32[]{:S(2)}) collective-permute-start(bf16[2,2,12,4096]{3,1,2,0:T(2,128)(2,1)S(1)} %get-tuple-element.9), channel_id=1, source_target_pairs={{0,0},{1,1},{2,8},{3,9},{4,16},{5,17},{6,24},{7,25},{8,2},{9,3},{1... | collective-permute-start | bytes 1179656 | tf_op jit(solution)/shard_map/ppermute | solution.py:70
  232.5 1.4 copy-start.3
  236.6 7.9 %copy-start.1 = (bf16[4,2,47,4096]{3,1,2,0:T(2,128)(2,1)S(1)}, bf16[4,2,47,4096]{3,1,2,0:T(2,128)(2,1)}, u32[]{:S(2)}) copy-start(bf16[4,2,47,4096]{3,1,2,0:T(2,128)(2,1)} %param.5) | copy-start | bytes 9240580
Sparse Core Ops, SparseCore 0:
  9.5 47.0 all-gather.1
